TPU v7x, 256 devices: a whole 4x4x8 slice. The times are simulated.
256 devices in a mesh: grp: 2 (over z_lo), gx: 64 (over x, z_hi, y), gz: 2 (over core).
Axes of the slice: x: 4, y: 4, z: 8 (z_hi: 4, z_lo: 2; z = z_hi * 2 + z_lo), core: 2. Of those that a mesh axis runs over, the one named last changes fastest.
Arguments:
- fields: float32 [4, 2, 4, 4096, 1024], P(None, 'grp', None, 'gx', 'gz'), may hold values from -4 to 4
- buoyancy: float32 [2, 4, 4096, 1024], P('grp', None, 'gx', 'gz'), may hold values from 0.3 to 0.9
- stiffness: float32 [2, 4, 4096, 1024], P('grp', None, 'gx', 'gz'), may hold values from 0.2 to 0.7
- stress_zero: float32 [4096, 1024], P('gx', 'gz'), may hold values from -5 to 5
- direct_effect: float32 [4096, 1024], P('gx', 'gz'), may hold values from 1 to 8
- log_state: float32 [4096, 1024], P('gx', 'gz'), may hold values from -2 to 2
- kernel: float32 [16, 1024, 4096], P(None, ('grp', 'gx', 'gz')), may hold values from -2 to 2
- history: float32 [16, 1024, 2, 4096], P(None, ('grp', 'gx', 'gz')), may hold values from -5 to 5
- truncation: int32 [1024, 4096], P(('grp', 'gx', 'gz')), may hold values from 1 to 16
Outputs:
- fields_next: float32 [4, 2, 4, 4096, 1024], P(None, 'grp', None, 'gx', 'gz')
- state_next: float32 [4096, 1024], P('gx', 'gz')
- spectra_new: float32 [4, 1024, 2, 4096], P(None, ('grp', 'gx', 'gz'))
All inputs are finite; a program needn't handle non-finite values.
Results may differ from a plain program's by a relative error of at most 0.0003.
Values sent between devices are 32-bit elements; how exact they have to be, the bound alone decides.
A program may use at most 128 MiB of HBM per device.

v0:
```python
import math
import jax
import jax.numpy as jnp
from jax import lax
from jax.sharding import PartitionSpec as P

NSTEP = 4
NEWTON = 4
FACE_NEAR = 9.0 / 8.0
FACE_FAR = 1.0 / 24.0
DAMPING = 1.0
FULL_PRECISION = lax.Precision.HIGHEST


def extended(cells, sides, width):
    for axis, dim in sides:
        count = lax.axis_size(axis)
        ends = count - 1
        head = lax.slice_in_dim(cells, 0, width, axis=dim)
        tail = lax.slice_in_dim(cells, cells.shape[dim] - width, cells.shape[dim], axis=dim)
        cells = jnp.concatenate(
            [
                lax.ppermute(tail, axis, [(i, (i + 1) % count) for i in range(ends)]),
                cells,
                lax.ppermute(head, axis, [((i + 1) % count, i) for i in range(ends)]),
            ],
            axis=dim,
        )
    return cells


def from_partner(x, axis, stride):
    return lax.ppermute(x, axis, [(i, i ^ 1 << stride) for i in range(lax.axis_size(axis))])


def stencil(values, axis_index, pad_before, pad_after):
    widths = [(0, 0)] * values.ndim
    widths[axis_index] = (pad_before, pad_after)
    padded = jnp.pad(values, widths)
    length = values.shape[axis_index]

    def window(offset):
        return lax.slice_in_dim(padded, offset, offset + length, axis=axis_index)

    return FACE_NEAR * (window(2) - window(1)) - FACE_FAR * (window(3) - window(0))


def margin_stencil(padded, axis_index, length, lead_cells):

    def window(offset):
        return lax.slice_in_dim(
            padded, lead_cells + offset, lead_cells + offset + length, axis=axis_index
        )

    return FACE_NEAR * (window(2) - window(1)) - FACE_FAR * (window(3) - window(0))


def inverse_sinh(scaled):
    magnitude = jnp.abs(scaled)
    positive = jnp.log(magnitude + jnp.sqrt(1.0 + magnitude * magnitude))
    return jnp.where(scaled < 0.0, -positive, positive)


def friction(loading, direct_effect, log_state, initial):
    factor = jnp.exp(log_state)
    slip_rate = initial
    for repeat in range(NEWTON):
        scaled = slip_rate * factor
        misfit = direct_effect * inverse_sinh(scaled) + DAMPING * slip_rate - loading
        slope_total = direct_effect * factor / jnp.sqrt(1.0 + scaled * scaled) + DAMPING
        slip_rate = slip_rate - misfit / slope_total
    return slip_rate


def phase_table(first_index, second_index, length, direction):
    turn_count = first_index * second_index % length
    angle_value = turn_count.astype(jnp.float32) * (2.0 * math.pi / length)
    return (jnp.cos(angle_value), direction * jnp.sin(angle_value))


def complex_apply(real_part, imag_part, cos_table, sin_table, formula):
    real_cos = jnp.einsum(formula, real_part, cos_table, precision=FULL_PRECISION)
    imag_sin = jnp.einsum(formula, imag_part, sin_table, precision=FULL_PRECISION)
    real_sin = jnp.einsum(formula, real_part, sin_table, precision=FULL_PRECISION)
    imag_cos = jnp.einsum(formula, imag_part, cos_table, precision=FULL_PRECISION)
    return (real_cos - imag_sin, real_sin + imag_cos)


def strike_forward(values, outer_count, inner_count):
    planes_count = values.shape[0]
    total_count = outer_count * inner_count
    real_part = values[:, 0].reshape(planes_count, outer_count, inner_count)
    imag_part = values[:, 1].reshape(planes_count, outer_count, inner_count)
    outer_iota = jnp.arange(outer_count, dtype=jnp.int32)
    inner_iota = jnp.arange(inner_count, dtype=jnp.int32)
    cos_table, sin_table = phase_table(outer_iota[:, None], outer_iota[None, :], outer_count, -1.0)
    real_part, imag_part = complex_apply(real_part, imag_part, cos_table, sin_table, "rab,ak->rkb")
    cos_table, sin_table = phase_table(outer_iota[:, None], inner_iota[None, :], total_count, -1.0)
    real_part, imag_part = (
        real_part * cos_table - imag_part * sin_table,
        real_part * sin_table + imag_part * cos_table,
    )
    cos_table, sin_table = phase_table(inner_iota[:, None], inner_iota[None, :], inner_count, -1.0)
    real_part, imag_part = complex_apply(real_part, imag_part, cos_table, sin_table, "rkb,bm->rmk")
    return jnp.stack(
        [
            real_part.reshape(planes_count, total_count),
            imag_part.reshape(planes_count, total_count),
        ],
        axis=1,
    )


def strike_inverse(values, outer_count, inner_count):
    planes_count = values.shape[0]
    total_count = outer_count * inner_count
    real_part = values[:, 0].reshape(planes_count, inner_count, outer_count)
    imag_part = values[:, 1].reshape(planes_count, inner_count, outer_count)
    outer_iota = jnp.arange(outer_count, dtype=jnp.int32)
    inner_iota = jnp.arange(inner_count, dtype=jnp.int32)
    cos_table, sin_table = phase_table(inner_iota[:, None], inner_iota[None, :], inner_count, 1.0)
    real_part, imag_part = complex_apply(real_part, imag_part, cos_table, sin_table, "rmk,mb->rkb")
    cos_table, sin_table = phase_table(outer_iota[:, None], inner_iota[None, :], total_count, 1.0)
    real_part, imag_part = (
        real_part * cos_table - imag_part * sin_table,
        real_part * sin_table + imag_part * cos_table,
    )
    cos_table, sin_table = phase_table(outer_iota[:, None], outer_iota[None, :], outer_count, 1.0)
    real_part, imag_part = complex_apply(real_part, imag_part, cos_table, sin_table, "rkb,ka->rab")
    return jnp.stack(
        [
            real_part.reshape(planes_count, total_count),
            imag_part.reshape(planes_count, total_count),
        ],
        axis=1,
    )


def per_device(
    fields, buoyancy, stiffness, stress_zero, direct_effect, log_state, kernel, history, truncation
):
    side_index = lax.axis_index("grp")
    on_plus = side_index == 1
    depth_index = lax.axis_index("gz")
    strike_devices = lax.axis_size("gx")
    depth_devices = lax.axis_size("gz")
    velocity = fields[0]
    normal_stress = fields[1]
    shear_stress = fields[2:4]
    strike_rows = velocity.shape[2]
    depth_cols = velocity.shape[3]
    modes_dev = history.shape[1]
    strike_total = history.shape[3]
    depth_total = depth_cols * depth_devices
    mode_rows = strike_devices * modes_dev
    scale_back = 1.0 / math.sqrt(strike_total * depth_total)
    lag_number = lax.broadcasted_iota(jnp.int32, kernel.shape, 0)
    weights = jnp.where(lag_number < truncation[None], kernel, jnp.zeros_like(kernel))

    def mode_numbers(row_index, depth_part):
        return (
            (side_index * strike_devices + row_index // modes_dev) * depth_devices + depth_part
        ) * modes_dev + row_index % modes_dev

    own_modes = mode_numbers(jnp.arange(mode_rows, dtype=jnp.int32), depth_index)
    depth_iota = jnp.arange(depth_total, dtype=jnp.int32)
    back_cos, back_sin = phase_table(own_modes[:, None], depth_iota[None, :], depth_total, 1.0)
    lagged = history
    spectra = []
    for step_number in range(NSTEP):
        summed = jnp.sum(weights[:, :, None, :] * lagged, axis=0)
        in_space = strike_inverse(summed, strike_devices, strike_rows)
        by_rows = lax.all_to_all(in_space, "gx", split_axis=2, concat_axis=0, tiled=True)
        partial_value = jnp.einsum(
            "jy,jz->yz", by_rows[:, 0], back_cos, precision=FULL_PRECISION
        ) - jnp.einsum("jy,jz->yz", by_rows[:, 1], back_sin, precision=FULL_PRECISION)
        own_depth = lax.psum_scatter(partial_value, "gz", scatter_dimension=1, tiled=True)
        relief = lax.psum(own_depth, "grp") * scale_back
        padded = extended(velocity, (("gx", 2), ("gz", 3)), 2)
        normal_stress = normal_stress + stiffness * stencil(velocity, 1, 2, 1)
        strike_grad = margin_stencil(padded[:, :, :, 2 : 2 + depth_cols], 2, strike_rows, 1)
        depth_grad = margin_stencil(padded[:, :, 2 : 2 + strike_rows, :], 3, depth_cols, 1)
        shear_stress = shear_stress + stiffness * jnp.stack([strike_grad, depth_grad])
        near_plane = velocity[0, 0]
        far_plane = from_partner(near_plane, "grp", 0)
        velocity_plus = jnp.where(on_plus, near_plane, far_plane)
        velocity_minus = jnp.where(on_plus, far_plane, near_plane)
        slip_guess = velocity_plus - velocity_minus
        loading = stress_zero + relief + DAMPING * slip_guess
        slip_rate = friction(loading, direct_effect, log_state, slip_guess)
        traction = loading - DAMPING * slip_rate
        log_state = 0.75 * log_state - 0.2 * jnp.log(1.0 + slip_rate * slip_rate) + 0.1
        normal_stress = normal_stress.at[0, 0].set(jnp.where(on_plus, traction, -traction))
        shear_rim = extended(shear_stress, (("gx", 3), ("gz", 4)), 2)
        strike_div = margin_stencil(shear_rim[0][:, :, :, 2 : 2 + depth_cols], 2, strike_rows, 0)
        depth_div = margin_stencil(shear_rim[1][:, :, 2 : 2 + strike_rows, :], 3, depth_cols, 0)
        velocity = velocity + buoyancy * (stencil(normal_stress, 1, 1, 2) + strike_div + depth_div)
        term_index = jnp.arange(mode_rows * lax.axis_size("gz"), dtype=jnp.int32)
        term_modes = mode_numbers(term_index % mode_rows, term_index // mode_rows)
        depth_here = depth_index * depth_cols + jnp.arange(depth_cols, dtype=jnp.int32)
        cos_part, sin_part = phase_table(
            term_modes[:, None], depth_here[None, :], depth_total, -1.0
        )
        real_term = jnp.einsum("jz,yz->jy", cos_part, slip_rate, precision=FULL_PRECISION)
        imag_term = jnp.einsum("jz,yz->jy", sin_part, slip_rate, precision=FULL_PRECISION)
        by_modes = lax.psum_scatter(
            jnp.stack([real_term, imag_term], axis=1), "gz", scatter_dimension=0, tiled=True
        )
        spread = lax.all_to_all(by_modes, "gx", split_axis=0, concat_axis=2, tiled=True)
        fresh_modes = strike_forward(spread, strike_devices, strike_rows) * scale_back
        spectra.append(fresh_modes)
        lagged = jnp.concatenate([fresh_modes[None], lagged[:-1]], axis=0)
    return (
        jnp.stack([velocity, normal_stress, shear_stress[0], shear_stress[1]]),
        log_state,
        jnp.stack(spectra),
    )


def solution(mesh):
    return jax.shard_map(
        per_device,
        mesh=mesh,
        in_specs=(
            P(None, "grp", None, "gx", "gz"),
            P("grp", None, "gx", "gz"),
            P("grp", None, "gx", "gz"),
            P("gx", "gz"),
            P("gx", "gz"),
            P("gx", "gz"),
            P(None, ("grp", "gx", "gz"), None),
            P(None, ("grp", "gx", "gz"), None, None),
            P(("grp", "gx", "gz"), None),
        ),
        out_specs=(
            P(None, "grp", None, "gx", "gz"),
            P("gx", "gz"),
            P(None, ("grp", "gx", "gz"), None, None),
        ),
        check_vma=False,
    )
```

profile of v0, /device:TPU:1, one launch (start us, length us, event | category | flops | bytes accessed | tf_op | source)
XLA Modules:
  0.0 803.6 jit_solution(6997939394833421156)
XLA Ops:
  9.7 4.6 collective-permute-start.2
  22.0 4.4 copy.238
  26.4 7.4 reshape.589
  33.9 18.6 %all-to-all-start = ((f32[64,1,512]{2,1,0:T(1,128)}), f32[64,1,512]{2,1,0:T(1,128)S(1)}, u32[]{:S(2)}, u32[]{:S(2)}) async-start(f32[64,1,512]{2,1,0:T(1,128)} %reshape.589), calls=%async_computation | async-start | bytes 262144 | tf_op jit(solution)/shard_map/all_to_all | solution.py:173
  69.9 7.9 reshape.590
  77.8 5.4 copy.332
  83.3 4.6 fusion.195
  88.0 5.4 convolution_subtract_fusion.3
  94.1 10.1 %collective-permute-start = (f32[64,512]{1,0:T(8,128)}, f32[64,512]{1,0:T(8,128)}, u32[]{:S(2)}, u32[]{:S(2)}) collective-permute-start(f32[64,512]{1,0:T(8,128)} %slice_bitcast_fusion.24), channel_id=1, source_target_pairs={{0,128},{128,0},{1,129},{129,1},{2,130},{130,2},{3,131},{131,3},{4... | collective-permute-start | bytes 393224 | tf_op jit(solution)/shard_map/ppermute | solution.py:33
  117.8 33.4 %all-reduce.13.cloned.1.call-done = f32[64,512]{1,0:T(8,128)} async-done(((f32[64,512]{1,0:T(8,128)}), f32[64,512]{1,0:T(8,128)}) %all-reduce.13.cloned.1.call-update) | async-done | bytes 131088 | tf_op jit(solution)/shard_map/psum | solution.py:178
  153.4 5.0 convolution_bitcast_fusion.6
  158.4 4.9 convolution_bitcast_fusion.7
  164.0 4.7 fusion.70
  175.6 5.2 collective-permute-start.12
  187.7 17.2 %all-to-all-start.1 = ((f32[64,1,512]{2,1,0:T(1,128)}), f32[64,1,512]{2,1,0:T(1,128)S(1)}, u32[]{:S(2)}, u32[]{:S(2)}) async-start(f32[64,1,512]{2,1,0:T(1,128)} %reshape.591), calls=%async_computation.3 | async-start | bytes 262144 | tf_op jit(solution)/shard_map/all_to_all | solution.py:209
  208.3 8.1 %all-to-all-done.1 = f32[64,1,512]{2,1,0:T(1,128)S(1)} async-done(((f32[64,1,512]{2,1,0:T(1,128)}), f32[64,1,512]{2,1,0:T(1,128)S(1)}, u32[]{:S(2)}, u32[]{:S(2)}) %all-to-all-start.1) | async-done | bytes 131104 | tf_op jit(solution)/shard_map/all_to_all | solution.py:209
  256.2 4.4 copy.256
  260.6 7.4 reshape.593
  268.0 4.6 all-to-all-start.2
  279.8 4.3 all-to-all-done.2
  285.0 8.0 reshape.594
  293.0 5.4 copy.337
  298.5 4.6 fusion.193
  303.1 5.4 convolution_subtract_fusion.2
  311.2 6.3 collective-permute-start.17
  321.3 4.2 reduce-scatter.13.cloned.1.call-done
  328.1 32.7 %all-reduce.15.cloned.1.call-done = f32[64,512]{1,0:T(8,128)} async-done(((f32[64,512]{1,0:T(8,128)}), f32[64,512]{1,0:T(8,128)}) %all-reduce.15.cloned.1.call-update) | async-done | bytes 131088 | tf_op jit(solution)/shard_map/psum | solution.py:178
  362.9 5.0 convolution_bitcast_fusion.4
  367.9 4.9 convolution_bitcast_fusion.5
  380.9 4.4 collective-permute-start.21
  391.2 7.4 reduce-scatter.15.cloned.1.call-done
  402.2 12.6 %all-to-all-start.3 = ((f32[64,1,512]{2,1,0:T(1,128)}), f32[64,1,512]{2,1,0:T(1,128)}, u32[]{:S(2)}, u32[]{:S(2)}) async-start(f32[64,1,512]{2,1,0:T(1,128)} %reshape.595), calls=%async_computation.7 | async-start | bytes 262144 | tf_op jit(solution)/shard_map/all_to_all | solution.py:209
  418.1 8.6 %all-to-all-done.3 = f32[64,1,512]{2,1,0:T(1,128)} async-done(((f32[64,1,512]{2,1,0:T(1,128)}), f32[64,1,512]{2,1,0:T(1,128)}, u32[]{:S(2)}, u32[]{:S(2)}) %all-to-all-start.3) | async-done | bytes 131104 | tf_op jit(solution)/shard_map/all_to_all | solution.py:209
  450.4 4.4 copy.272
  454.8 7.5 reshape.597
  462.3 5.5 all-to-all-start.4
  480.8 8.3 %reshape.598 = f32[4096,2,4]{2,1,0:T(2,128)} reshape(f32[64,512]{1,0:T(8,128)S(1)} %reduce.44) | data formatting | bytes 262144
  489.1 5.4 copy.342
  494.7 4.6 fusion.191
  499.3 5.4 convolution_subtract_fusion.1
  507.4 4.6 collective-permute-start.26
  516.1 4.9 reduce-scatter.17.cloned.1.call-done
  523.7 32.8 %all-reduce.17.cloned.1.call-done = f32[64,512]{1,0:T(8,128)} async-done(((f32[64,512]{1,0:T(8,128)}), f32[64,512]{1,0:T(8,128)}) %all-reduce.17.cloned.1.call-update) | async-done | bytes 131088 | tf_op jit(solution)/shard_map/psum | solution.py:178
  558.7 5.0 convolution_bitcast_fusion.2
  563.7 4.9 convolution_bitcast_fusion.3
  569.3 4.7 fusion.102
  581.2 5.3 collective-permute-start.30
  588.4 17.2 %all-to-all-start.5 = ((f32[64,1,512]{2,1,0:T(1,128)}), f32[64,1,512]{2,1,0:T(1,128)S(1)}, u32[]{:S(2)}, u32[]{:S(2)}) async-start(f32[64,1,512]{2,1,0:T(1,128)} %reshape.599), calls=%async_computation.11 | async-start | bytes 262144 | tf_op jit(solution)/shard_map/all_to_all | solution.py:209
  612.3 5.3 all-to-all-done.5
  635.3 4.4 copy.288
  639.7 7.5 reshape.601
  647.2 6.9 all-to-all-start.6
  656.8 8.7 %all-to-all-done.6 = f32[64,1,512]{2,1,0:T(1,128)S(1)} async-done(((f32[64,1,512]{2,1,0:T(1,128)}), f32[64,1,512]{2,1,0:T(1,128)S(1)}, u32[]{:S(2)}, u32[]{:S(2)}) %all-to-all-start.6) | async-done | bytes 131104 | tf_op jit(solution)/shard_map/all_to_all | solution.py:173
  666.5 7.9 reshape.602
  674.4 5.4 copy.347
  679.9 4.6 fusion.189
  684.6 5.4 convolution_subtract_fusion
  702.5 6.5 collective-permute-start.35
  709.1 25.8 %all-reduce.19.cloned.1.call-done = f32[64,512]{1,0:T(8,128)} async-done(((f32[64,512]{1,0:T(8,128)}), f32[64,512]{1,0:T(8,128)}) %all-reduce.19.cloned.1.call-update) | async-done | bytes 131088 | tf_op jit(solution)/shard_map/psum | solution.py:178
  737.1 5.0 convolution_bitcast_fusion
  742.1 4.9 convolution_bitcast_fusion.1
  750.1 12.4 %reduce-scatter.23.cloned.1.call-done = f32[256,2,64]{0,2,1:T(8,128)} async-done(((f32[512,2,64]{0,2,1:T(8,128)}), f32[256,2,64]{0,2,1:T(8,128)}) %reduce-scatter.23.cloned.1.call-update) | async-done | bytes 131088 | tf_op jit(solution)/shard_map/reduce_scatter | solution.py:206
  764.5 12.3 %all-to-all-start.7 = ((f32[64,1,512]{2,1,0:T(1,128)}), f32[64,1,512]{2,1,0:T(1,128)S(1)}, u32[]{:S(2)}, u32[]{:S(2)}) async-start(f32[64,1,512]{2,1,0:T(1,128)} %reshape.603), calls=%async_computation.15 | async-start | bytes 262144 | tf_op jit(solution)/shard_map/all_to_all | solution.py:209
  783.2 5.7 all-to-all-done.7
  (413 shorter events, 261.2 us)
Async XLA Ops:
  8.4 44.1 %collective-permute-start.1 = (f32[1,4,2,512]{3,2,1,0:T(2,128)S(1)}, f32[1,4,2,512]{3,2,1,0:T(2,128)S(1)}, u32[]{:S(2)}, u32[]{:S(2)}) collective-permute-start(f32[1,4,2,512]{3,2,1,0:T(2,128)S(1)} %get-tuple-element.127), channel_id=1, source_target_pairs={{2,0},{4,2},{6,4},{8,6},{10,8},{12,10},{14,12},{16,14},{18,16},{20... | collective-permute-start | bytes 49160 | tf_op jit(solution)/shard_map/ppermute | solution.py:25
  9.7 42.8 %collective-permute-start.2 = (f32[1,4,2,512]{3,2,1,0:T(2,128)S(1)}, f32[1,4,2,512]{3,2,1,0:T(2,128)S(1)}, u32[]{:S(2)}, u32[]{:S(2)}) collective-permute-start(f32[1,4,2,512]{3,2,1,0:T(2,128)S(1)} %get-tuple-element.126), channel_id=1, source_target_pairs={{0,2},{2,4},{4,6},{6,8},{8,10},{10,12},{12,14},{14,16},{16,18},{18... | collective-permute-start | bytes 49160 | tf_op jit(solution)/shard_map/ppermute | solution.py:23
  33.9 34.6 %all-to-all-start = ((f32[64,1,512]{2,1,0:T(1,128)}), f32[64,1,512]{2,1,0:T(1,128)S(1)}, u32[]{:S(2)}, u32[]{:S(2)}) async-start(f32[64,1,512]{2,1,0:T(1,128)} %reshape.589), calls=%async_computation | async-start | bytes 262144 | tf_op jit(solution)/shard_map/all_to_all | solution.py:173
  52.5 62.6 %reduce-scatter.9.cloned.1.call-start = ((), (), s32[]{:S(2)}) async-start(), calls=%async_computation.16 | async-start | bytes 393216 | tf_op jit(solution)/shard_map/reduce_scatter | solution.py:177
  52.7 4.7 collective-permute-start.3
  56.1 3.3 collective-permute-start.4
  61.8 210.9 %copy-start.2 = (f32[1,1,4,64,512]{4,3,2,1,0:T(8,128)}, f32[1,1,4,64,512]{4,3,2,1,0:T(8,128)S(1)}, u32[]{:S(2)}) copy-start(f32[1,1,4,64,512]{4,3,2,1,0:T(8,128)S(1)} %get-tuple-element.113) | copy-start | bytes 1572868
  63.7 40.4 %collective-permute-start.5 = (f32[2,1,4,2,512]{4,3,2,1,0:T(2,128)}, f32[2,1,4,2,512]{4,3,2,1,0:T(2,128)S(1)}, u32[]{:S(2)}, u32[]{:S(2)}) collective-permute-start(f32[2,1,4,2,512]{4,3,2,1,0:T(2,128)} %get-tuple-element.98), channel_id=1, source_target_pairs={{0,2},{2,4},{4,6},{6,8},{8,10},{10,12},{12,14},{14,16},{16,18},{18... | collective-permute-start | bytes 98312 | tf_op jit(solution)/shard_map/ppermute | solution.py:23
  66.9 37.2 %collective-permute-start.6 = (f32[2,1,4,2,512]{4,3,2,1,0:T(2,128)}, f32[2,1,4,2,512]{4,3,2,1,0:T(2,128)S(1)}, u32[]{:S(2)}, u32[]{:S(2)}) collective-permute-start(f32[2,1,4,2,512]{4,3,2,1,0:T(2,128)} %get-tuple-element.99), channel_id=1, source_target_pairs={{2,0},{4,2},{6,4},{8,6},{10,8},{12,10},{14,12},{16,14},{18,16},{20... | collective-permute-start | bytes 98312 | tf_op jit(solution)/shard_map/ppermute | solution.py:25
  93.4 57.8 %all-reduce.13.cloned.1.call-start = ((), (), s32[]{:S(2)}) async-start(), calls=%async_computation.17 | async-start | bytes 262144 | tf_op jit(solution)/shard_map/psum | solution.py:178
  94.1 23.7 %collective-permute-start = (f32[64,512]{1,0:T(8,128)}, f32[64,512]{1,0:T(8,128)}, u32[]{:S(2)}, u32[]{:S(2)}) collective-permute-start(f32[64,512]{1,0:T(8,128)} %slice_bitcast_fusion.24), channel_id=1, source_target_pairs={{0,128},{128,0},{1,129},{129,1},{2,130},{130,2},{3,131},{131,3},{4... | collective-permute-start | bytes 393224 | tf_op jit(solution)/shard_map/ppermute | solution.py:33
  106.2 5.1 collective-permute-start.7
  107.4 4.6 collective-permute-start.8
  115.2 70.6 %reduce-scatter.11.cloned.1.call-start = ((), (), s32[]{:S(2)}) async-start(), calls=%async_computation.18 | async-start | bytes 393216 | tf_op jit(solution)/shard_map/reduce_scatter | solution.py:206
  168.7 5.3 collective-permute-start.10
  170.0 4.8 collective-permute-start.11
  175.6 8.3 %collective-permute-start.12 = (f32[1,4,68,2]{3,2,1,0:T(8,128)S(1)}, f32[1,4,68,2]{3,2,1,0:T(8,128)}, u32[]{:S(2)}, u32[]{:S(2)}) collective-permute-start(f32[1,4,68,2]{3,2,1,0:T(8,128)S(1)} %get-tuple-element.110), channel_id=1, source_target_pairs={{1,0},{3,2},{5,4},{7,6},{9,8},{11,10},{13,12},{15,14},{17,16},{19,... | collective-permute-start | bytes 6536 | tf_op jit(solution)/shard_map/ppermute | solution.py:25
  182.6 22.4 %collective-permute-start.13 = (f32[1,4,68,2]{3,2,1,0:T(8,128)}, f32[1,4,68,2]{3,2,1,0:T(8,128)}, u32[]{:S(2)}, u32[]{:S(2)}) collective-permute-start(f32[1,4,68,2]{3,2,1,0:T(8,128)} %get-tuple-element.111), channel_id=1, source_target_pairs={{0,1},{2,3},{4,5},{6,7},{8,9},{10,11},{12,13},{14,15},{16,17},{18,... | collective-permute-start | bytes 6536 | tf_op jit(solution)/shard_map/ppermute | solution.py:23
  187.7 28.6 %all-to-all-start.1 = ((f32[64,1,512]{2,1,0:T(1,128)}), f32[64,1,512]{2,1,0:T(1,128)S(1)}, u32[]{:S(2)}, u32[]{:S(2)}) async-start(f32[64,1,512]{2,1,0:T(1,128)} %reshape.591), calls=%async_computation.3 | async-start | bytes 262144 | tf_op jit(solution)/shard_map/all_to_all | solution.py:209
  268.0 16.0 %all-to-all-start.2 = ((f32[64,1,512]{2,1,0:T(1,128)}), f32[64,1,512]{2,1,0:T(1,128)S(1)}, u32[]{:S(2)}, u32[]{:S(2)}) async-start(f32[64,1,512]{2,1,0:T(1,128)} %reshape.593), calls=%async_computation.4 | async-start | bytes 262144 | tf_op jit(solution)/shard_map/all_to_all | solution.py:173
  272.6 52.8 %reduce-scatter.13.cloned.1.call-start = ((), (), s32[]{:S(2)}) async-start(), calls=%async_computation.19 | async-start | bytes 393216 | tf_op jit(solution)/shard_map/reduce_scatter | solution.py:177
  275.7 32.9 %collective-permute-start.14 = (f32[2,1,4,2,512]{4,3,2,1,0:T(2,128)S(1)}, f32[2,1,4,2,512]{4,3,2,1,0:T(2,128)S(1)}, u32[]{:S(2)}, u32[]{:S(2)}) collective-permute-start(f32[2,1,4,2,512]{4,3,2,1,0:T(2,128)S(1)} %get-tuple-element.96), channel_id=1, source_target_pairs={{0,2},{2,4},{4,6},{6,8},{8,10},{10,12},{12,14},{14,16},{16,18},{18... | collective-permute-start | bytes 98312 | tf_op jit(solution)/shard_map/ppermute | solution.py:23
  278.5 30.1 %collective-permute-start.15 = (f32[2,1,4,2,512]{4,3,2,1,0:T(2,128)S(1)}, f32[2,1,4,2,512]{4,3,2,1,0:T(2,128)S(1)}, u32[]{:S(2)}, u32[]{:S(2)}) collective-permute-start(f32[2,1,4,2,512]{4,3,2,1,0:T(2,128)S(1)} %get-tuple-element.97), channel_id=1, source_target_pairs={{2,0},{4,2},{6,4},{8,6},{10,8},{12,10},{14,12},{16,14},{18,16},{20... | collective-permute-start | bytes 98312 | tf_op jit(solution)/shard_map/ppermute | solution.py:25
  308.5 52.2 %all-reduce.15.cloned.1.call-start = ((), (), s32[]{:S(2)}) async-start(), calls=%async_computation.20 | async-start | bytes 262144 | tf_op jit(solution)/shard_map/psum | solution.py:178
  309.9 8.8 %collective-permute-start.16 = (f32[2,1,4,68,2]{4,3,2,1,0:T(8,128)S(1)}, f32[2,1,4,68,2]{4,3,2,1,0:T(8,128)S(1)}, u32[]{:S(2)}, u32[]{:S(2)}) collective-permute-start(f32[2,1,4,68,2]{4,3,2,1,0:T(8,128)S(1)} %get-tuple-element.88), channel_id=1, source_target_pairs={{0,1},{2,3},{4,5},{6,7},{8,9},{10,11},{12,13},{14,15},{16,17},{18,... | collective-permute-start | bytes 13064 | tf_op jit(solution)/shard_map/ppermute | solution.py:23
  311.2 7.5 collective-permute-start.17
  317.5 10.5 %collective-permute-start.9 = (f32[64,512]{1,0:T(8,128)S(1)}, f32[64,512]{1,0:T(8,128)S(1)}, u32[]{:S(2)}, u32[]{:S(2)}) collective-permute-start(f32[64,512]{1,0:T(8,128)S(1)} %slice_bitcast_fusion.19), channel_id=1, source_target_pairs={{0,128},{128,0},{1,129},{129,1},{2,130},{130,2},{3,131},{131,3},{4... | collective-permute-start | bytes 393224 | tf_op jit(solution)/shard_map/ppermute | solution.py:33
  325.5 73.1 %reduce-scatter.15.cloned.1.call-start = ((), (), s32[]{:S(2)}) async-start(), calls=%async_computation.21 | async-start | bytes 393216 | tf_op jit(solution)/shard_map/reduce_scatter | solution.py:206
  373.9 6.1 collective-permute-start.19
  375.2 4.8 collective-permute-start.20
  380.9 9.4 %collective-permute-start.21 = (f32[1,4,68,2]{3,2,1,0:T(8,128)S(1)}, f32[1,4,68,2]{3,2,1,0:T(8,128)S(1)}, u32[]{:S(2)}, u32[]{:S(2)}) collective-permute-start(f32[1,4,68,2]{3,2,1,0:T(8,128)S(1)} %get-tuple-element.106), channel_id=1, source_target_pairs={{1,0},{3,2},{5,4},{7,6},{9,8},{11,10},{13,12},{15,14},{17,16},{19,... | collective-permute-start | bytes 6536 | tf_op jit(solution)/shard_map/ppermute | solution.py:25
  388.8 26.0 %collective-permute-start.22 = (f32[1,4,68,2]{3,2,1,0:T(8,128)}, f32[1,4,68,2]{3,2,1,0:T(8,128)}, u32[]{:S(2)}, u32[]{:S(2)}) collective-permute-start(f32[1,4,68,2]{3,2,1,0:T(8,128)} %get-tuple-element.107), channel_id=1, source_target_pairs={{0,1},{2,3},{4,5},{6,7},{8,9},{10,11},{12,13},{14,15},{16,17},{18,... | collective-permute-start | bytes 6536 | tf_op jit(solution)/shard_map/ppermute | solution.py:23
  402.2 24.5 %all-to-all-start.3 = ((f32[64,1,512]{2,1,0:T(1,128)}), f32[64,1,512]{2,1,0:T(1,128)}, u32[]{:S(2)}, u32[]{:S(2)}) async-start(f32[64,1,512]{2,1,0:T(1,128)} %reshape.595), calls=%async_computation.7 | async-start | bytes 262144 | tf_op jit(solution)/shard_map/all_to_all | solution.py:209
  462.3 16.7 %all-to-all-start.4 = ((f32[64,1,512]{2,1,0:T(1,128)}), f32[64,1,512]{2,1,0:T(1,128)}, u32[]{:S(2)}, u32[]{:S(2)}) async-start(f32[64,1,512]{2,1,0:T(1,128)} %reshape.597), calls=%async_computation.8 | async-start | bytes 262144 | tf_op jit(solution)/shard_map/all_to_all | solution.py:173
  467.7 53.3 %reduce-scatter.17.cloned.1.call-start = ((), (), s32[]{:S(2)}) async-start(), calls=%async_computation.22 | async-start | bytes 393216 | tf_op jit(solution)/shard_map/reduce_scatter | solution.py:177
  471.8 32.9 %collective-permute-start.23 = (f32[2,1,4,2,512]{4,3,2,1,0:T(2,128)}, f32[2,1,4,2,512]{4,3,2,1,0:T(2,128)S(1)}, u32[]{:S(2)}, u32[]{:S(2)}) collective-permute-start(f32[2,1,4,2,512]{4,3,2,1,0:T(2,128)} %get-tuple-element.94), channel_id=1, source_target_pairs={{0,2},{2,4},{4,6},{6,8},{8,10},{10,12},{12,14},{14,16},{16,18},{18... | collective-permute-start | bytes 98312 | tf_op jit(solution)/shard_map/ppermute | solution.py:23
  474.6 30.2 %collective-permute-start.24 = (f32[2,1,4,2,512]{4,3,2,1,0:T(2,128)}, f32[2,1,4,2,512]{4,3,2,1,0:T(2,128)}, u32[]{:S(2)}, u32[]{:S(2)}) collective-permute-start(f32[2,1,4,2,512]{4,3,2,1,0:T(2,128)} %get-tuple-element.95), channel_id=1, source_target_pairs={{2,0},{4,2},{6,4},{8,6},{10,8},{12,10},{14,12},{16,14},{18,16},{20... | collective-permute-start | bytes 98312 | tf_op jit(solution)/shard_map/ppermute | solution.py:25
  504.7 51.8 %all-reduce.17.cloned.1.call-start = ((), (), s32[]{:S(2)}) async-start(), calls=%async_computation.23 | async-start | bytes 262144 | tf_op jit(solution)/shard_map/psum | solution.py:178
  506.1 7.4 collective-permute-start.25
  507.4 6.2 collective-permute-start.26
  512.7 11.0 %collective-permute-start.18 = (f32[64,512]{1,0:T(8,128)}, f32[64,512]{1,0:T(8,128)}, u32[]{:S(2)}, u32[]{:S(2)}) collective-permute-start(f32[64,512]{1,0:T(8,128)} %slice_bitcast_fusion.14), channel_id=1, source_target_pairs={{0,128},{128,0},{1,129},{129,1},{2,130},{130,2},{3,131},{131,3},{4... | collective-permute-start | bytes 393224 | tf_op jit(solution)/shard_map/ppermute | solution.py:33
  516.1 40.4 %copy-start.29 = (f32[64,512]{1,0:T(8,128)S(1)}, f32[64,512]{1,0:T(8,128)}, u32[]{:S(2)}) copy-start(f32[64,512]{1,0:T(8,128)} %param.21) | copy-start | bytes 393220
  516.1 40.4 %copy-start.36 = (f32[64,512]{1,0:T(8,128)S(1)}, f32[64,512]{1,0:T(8,128)}, u32[]{:S(2)}) copy-start(f32[64,512]{1,0:T(8,128)} %param.22) | copy-start | bytes 393220
  516.1 40.4 %copy-start.39 = (f32[64,512]{1,0:T(8,128)S(1)}, f32[64,512]{1,0:T(8,128)}, u32[]{:S(2)}) copy-start(f32[64,512]{1,0:T(8,128)} %copy-done.37) | copy-start | bytes 393220
  516.1 40.4 %copy-start.44 = (f32[64,512]{1,0:T(8,128)S(1)}, f32[64,512]{1,0:T(8,128)}, u32[]{:S(2)}) copy-start(f32[64,512]{1,0:T(8,128)} %copy-done.43) | copy-start | bytes 393220
  521.1 65.3 %reduce-scatter.19.cloned.1.call-start = ((), (), s32[]{:S(2)}) async-start(), calls=%async_computation.24 | async-start | bytes 393216 | tf_op jit(solution)/shard_map/reduce_scatter | solution.py:206
  574.1 5.4 collective-permute-start.28
  575.5 4.8 collective-permute-start.29
  581.2 29.3 %collective-permute-start.30 = (f32[1,4,68,2]{3,2,1,0:T(8,128)}, f32[1,4,68,2]{3,2,1,0:T(8,128)}, u32[]{:S(2)}, u32[]{:S(2)}) collective-permute-start(f32[1,4,68,2]{3,2,1,0:T(8,128)} %get-tuple-element.102), channel_id=1, source_target_pairs={{1,0},{3,2},{5,4},{7,6},{9,8},{11,10},{13,12},{15,14},{17,16},{19,... | collective-permute-start | bytes 6536 | tf_op jit(solution)/shard_map/ppermute | solution.py:25
  588.4 29.2 %all-to-all-start.5 = ((f32[64,1,512]{2,1,0:T(1,128)}), f32[64,1,512]{2,1,0:T(1,128)S(1)}, u32[]{:S(2)}, u32[]{:S(2)}) async-start(f32[64,1,512]{2,1,0:T(1,128)} %reshape.599), calls=%async_computation.11 | async-start | bytes 262144 | tf_op jit(solution)/shard_map/all_to_all | solution.py:209
  609.2 45.0 %collective-permute-start.31 = (f32[1,4,68,2]{3,2,1,0:T(8,128)}, f32[1,4,68,2]{3,2,1,0:T(8,128)}, u32[]{:S(2)}, u32[]{:S(2)}) collective-permute-start(f32[1,4,68,2]{3,2,1,0:T(8,128)} %get-tuple-element.103), channel_id=1, source_target_pairs={{0,1},{2,3},{4,5},{6,7},{8,9},{10,11},{12,13},{14,15},{16,17},{18,... | collective-permute-start | bytes 6536 | tf_op jit(solution)/shard_map/ppermute | solution.py:23
  647.2 18.4 %all-to-all-start.6 = ((f32[64,1,512]{2,1,0:T(1,128)}), f32[64,1,512]{2,1,0:T(1,128)S(1)}, u32[]{:S(2)}, u32[]{:S(2)}) async-start(f32[64,1,512]{2,1,0:T(1,128)} %reshape.601), calls=%async_computation.12 | async-start | bytes 262144 | tf_op jit(solution)/shard_map/all_to_all | solution.py:173
  654.1 45.3 %reduce-scatter.21.cloned.1.call-start = ((), (), s32[]{:S(2)}) async-start(), calls=%async_computation.25 | async-start | bytes 393216 | tf_op jit(solution)/shard_map/reduce_scatter | solution.py:177
  690.0 44.9 %all-reduce.19.cloned.1.call-start = ((), (), s32[]{:S(2)}) async-start(), calls=%async_computation.26 | async-start | bytes 262144 | tf_op jit(solution)/shard_map/psum | solution.py:178
  693.1 41.8 %copy-start.30 = (f32[64,512]{1,0:T(8,128)S(1)}, f32[64,512]{1,0:T(8,128)}, u32[]{:S(2)}) copy-start(f32[64,512]{1,0:T(8,128)} %param.21) | copy-start | bytes 393220
  693.1 41.8 %copy-start.46 = (f32[64,512]{1,0:T(8,128)S(1)}, f32[64,512]{1,0:T(8,128)}, u32[]{:S(2)}) copy-start(f32[64,512]{1,0:T(8,128)} %copy-done.45) | copy-start | bytes 393220
  693.2 41.8 %copy-start.47 = (f32[64,512]{1,0:T(8,128)S(1)}, f32[64,512]{1,0:T(8,128)}, u32[]{:S(2)}) copy-start(f32[64,512]{1,0:T(8,128)} %get-tuple-element.71) | copy-start | bytes 393220
  693.2 6.3 collective-permute-start.32
  695.6 4.7 collective-permute-start.33
  696.9 12.1 %collective-permute-start.27 = (f32[64,512]{1,0:T(8,128)S(1)}, f32[64,512]{1,0:T(8,128)S(1)}, u32[]{:S(2)}, u32[]{:S(2)}) collective-permute-start(f32[64,512]{1,0:T(8,128)S(1)} %slice_bitcast_fusion.9), channel_id=1, source_target_pairs={{0,128},{128,0},{1,129},{129,1},{2,130},{130,2},{3,131},{131,3},{4... | collective-permute-start | bytes 393224 | tf_op jit(solution)/shard_map/ppermute | solution.py:33
  699.5 63.0 %reduce-scatter.23.cloned.1.call-start = ((), (), s32[]{:S(2)}) async-start(), calls=%async_computation.27 | async-start | bytes 393216 | tf_op jit(solution)/shard_map/reduce_scatter | solution.py:206
  701.2 46.5 %collective-permute-start.34 = (f32[2,1,4,68,2]{4,3,2,1,0:T(8,128)}, f32[2,1,4,68,2]{4,3,2,1,0:T(8,128)S(1)}, u32[]{:S(2)}, u32[]{:S(2)}) collective-permute-start(f32[2,1,4,68,2]{4,3,2,1,0:T(8,128)} %get-tuple-element.84), channel_id=1, source_target_pairs={{0,1},{2,3},{4,5},{6,7},{8,9},{10,11},{12,13},{14,15},{16,17},{18,... | collective-permute-start | bytes 13064 | tf_op jit(solution)/shard_map/ppermute | solution.py:23
  702.5 45.2 %collective-permute-start.35 = (f32[2,1,4,68,2]{4,3,2,1,0:T(8,128)}, f32[2,1,4,68,2]{4,3,2,1,0:T(8,128)S(1)}, u32[]{:S(2)}, u32[]{:S(2)}) collective-permute-start(f32[2,1,4,68,2]{4,3,2,1,0:T(8,128)} %get-tuple-element.85), channel_id=1, source_target_pairs={{1,0},{3,2},{5,4},{7,6},{9,8},{11,10},{13,12},{15,14},{17,16},{19,... | collective-permute-start | bytes 13064 | tf_op jit(solution)/shard_map/ppermute | solution.py:25
  764.5 24.4 %all-to-all-start.7 = ((f32[64,1,512]{2,1,0:T(1,128)}), f32[64,1,512]{2,1,0:T(1,128)S(1)}, u32[]{:S(2)}, u32[]{:S(2)}) async-start(f32[64,1,512]{2,1,0:T(1,128)} %reshape.603), calls=%async_computation.15 | async-start | bytes 262144 | tf_op jit(solution)/shard_map/all_to_all | solution.py:209
  (42 other events, 520.2 us)
Sparse Core Ops, SparseCore 0:
  93.5 17.6 reduce-scatter.8
  115.3 35.8 all-reduce.12
  164.1 14.6 reduce-scatter.10
  308.6 16.7 reduce-scatter.12
  327.8 32.8 all-reduce.14
  380.1 18.4 reduce-scatter.14
  504.8 16.1 reduce-scatter.16
  523.6 32.8 all-reduce.16
  569.5 14.6 reduce-scatter.18
  690.1 9.2 reduce-scatter.20
  702.0 32.8 all-reduce.18
  747.8 14.6 reduce-scatter.22
where the time goes:
time: 815 us; the launch traced here: 804 us
  waiting for transfers between devices  205 us (25%)
  starting transfers between devices  197 us (24%)
  local copies, waits for them, and re-layouts  159 us (20%)
  matrix products  123 us (15%)
  other arithmetic  104 us (13%)
  between operations  16.4 us (2%)
    psum x4, waiting for transfers between devices, per_device(): relief = lax.psum(own_depth, 'grp') * scale_back  125 us
    unnamed x116, local copies, waits for them, and re-layouts  73.8 us
    all_to_all x4, starting transfers between devices, per_device(): lax.all_to_all(by_modes, 'gx', split_axis=0, concat_axis=2, tiled=True)  59.3 us
    ppermute x16, starting transfers between devices, extended(): lax.ppermute(head, axis, [((i + 1) % count, i) for i in range(ends)])  50.3 us
    ppermute x16, starting transfers between devices, extended(): lax.ppermute(tail, axis, [(i, (i + 1) % count) for i in range(ends)])  38.2 us
    all_to_all x4, starting transfers between devices, per_device(): lax.all_to_all(in_space, 'gx', split_axis=2, concat_axis=0, tiled=True)  35.7 us
    all_to_all x4, waiting for transfers between devices, per_device(): lax.all_to_all(by_modes, 'gx', split_axis=0, concat_axis=2, tiled=True)  27.6 us
    all_to_all x9, local copies, waits for them, and re-layouts, per_device(): lax.all_to_all(in_space, 'gx', split_axis=2, concat_axis=0, tiled=True)  22.7 us
  transfers between devices with their start and end apart: 56, of which 22 were waited for; matrix products, arithmetic and copies ran while one was open for 28% of the time, Pallas kernels for 0%

commit v1 on v0

--- a/solution.py
+++ b/solution.py
@@ -175,7 +175,7 @@
             "jy,jz->yz", by_rows[:, 0], back_cos, precision=FULL_PRECISION
         ) - jnp.einsum("jy,jz->yz", by_rows[:, 1], back_sin, precision=FULL_PRECISION)
         own_depth = lax.psum_scatter(partial_value, "gz", scatter_dimension=1, tiled=True)
-        relief = lax.psum(own_depth, "grp") * scale_back
+        relief = jnp.sum(lax.all_gather(own_depth, "grp"), axis=0) * scale_back
         padded = extended(velocity, (("gx", 2), ("gz", 3)), 2)
         normal_stress = normal_stress + stiffness * stencil(velocity, 1, 2, 1)
         strike_grad = margin_stencil(padded[:, :, :, 2 : 2 + depth_cols], 2, strike_rows, 1)

time: 815 us -> 740 us (0.908)
  waiting for transfers between devices: 205 us -> 137 us
  blocking collectives: 0 us -> 37.9 us
  starting transfers between devices: 197 us -> 175 us
  matrix products: 123 us -> 111 us
    psum x4 -> x0, waiting for transfers between devices: 125 us -> none  [per_device(): relief = lax.psum(own_depth, 'grp') * scale_back]
    reduce_scatter x4, waiting for transfers between devices: 11 us -> 51 us  [per_device(): lax.psum_scatter(partial_value, 'gz', scatter_dimension=1, tiled=True)]
    all_gather x0 -> x4, blocking collectives: none -> 37.9 us  [per_device(): relief = jnp.sum(lax.all_gather(own_depth, 'grp'), axis=0) * scale_back]
    ppermute x16, waiting for transfers between devices: 1.57 us -> 12.7 us  [extended(): lax.ppermute(head, axis, [((i + 1) % count, i) for i in range(ends)])]
    ppermute x4, starting transfers between devices: 12.7 us -> 3.45 us  [from_partner(): lax.ppermute(x, axis, [(i, i ^ 1 << stride) for i in range(lax.axis_size(...]
    reduce_scatter x4, waiting for transfers between devices: 19.8 us -> 28.7 us  [per_device(): lax.psum_scatter(jnp.stack([real_term, imag_term], axis=1), 'gz', scatter...]
    unnamed x116 -> x122, local copies, waits for them, and re-layouts: 73.8 us -> 70.3 us
  transfers between devices with their start and end apart: 56 -> 52, of which waited for: 22 -> 22; matrix products, arithmetic and copies ran while one was open for 28% -> 22% of each run, Pallas kernels for 0% -> 0%
where the time goes in v1:
time: 740 us; the launch traced here: 728 us
  starting transfers between devices  175 us (24%)
  local copies, waits for them, and re-layouts  151 us (20%)
  waiting for transfers between devices  137 us (19%)
  matrix products  111 us (15%)
  other arithmetic  98.7 us (13%)
  blocking collectives  37.9 us (5%)
  between operations  16.6 us (2%)
    unnamed x122, local copies, waits for them, and re-layouts  70.3 us
    all_to_all x4, starting transfers between devices, per_device(): lax.all_to_all(by_modes, 'gx', split_axis=0, concat_axis=2, tiled=True)  53.3 us
    reduce_scatter x4, waiting for transfers between devices, per_device(): lax.psum_scatter(partial_value, 'gz', scatter_dimension=1, tiled=True)  51 us
    ppermute x16, starting transfers between devices, extended(): lax.ppermute(head, axis, [((i + 1) % count, i) for i in range(ends)])  49.8 us
    ppermute x16, starting transfers between devices, extended(): lax.ppermute(tail, axis, [(i, (i + 1) % count) for i in range(ends)])  38.3 us
    all_gather x4, blocking collectives, per_device(): relief = jnp.sum(lax.all_gather(own_depth, 'grp'), axis=0) * scale_back  37.9 us
    all_to_all x4, waiting for transfers between devices, per_device(): lax.all_to_all(by_modes, 'gx', split_axis=0, concat_axis=2, tiled=True)  31.6 us
    all_to_all x4, starting transfers between devices, per_device(): lax.all_to_all(in_space, 'gx', split_axis=2, concat_axis=0, tiled=True)  30.1 us
  transfers between devices with their start and end apart: 52, of which 22 were waited for; matrix products, arithmetic and copies ran while one was open for 22% of the time, Pallas kernels for 0%

profile of v1, /device:TPU:1, one launch (start us, length us, event | category | flops | bytes accessed | tf_op | source)
XLA Modules:
  0.0 728.1 jit_solution(5505913111794437823)
XLA Ops:
  15.0 4.3 copy.238
  19.3 7.4 %reshape.593 = f32[64,1,512]{2,1,0:T(1,128)} reshape(f32[4096,2,4]{2,1,0:T(2,128)} %bitcast.433) | data formatting | bytes 262144
  26.7 15.2 %all-to-all-start = ((f32[64,1,512]{2,1,0:T(1,128)}), f32[64,1,512]{2,1,0:T(1,128)S(1)}, u32[]{:S(2)}, u32[]{:S(2)}) async-start(f32[64,1,512]{2,1,0:T(1,128)} %reshape.593), calls=%async_computation | async-start | bytes 262144 | tf_op jit(solution)/shard_map/all_to_all | solution.py:173
  44.4 4.0 collective-permute-start.2
  72.2 4.9 collective-permute-start.8
  78.6 7.8 %reshape.594 = f32[4096,2,4]{2,1,0:T(2,128)} reshape(f32[64,512]{1,0:T(8,128)S(1)} %reduce.40) | data formatting | bytes 262144
  86.5 5.4 copy.332
  92.0 4.6 fusion.195
  96.6 5.4 convolution_subtract_fusion.3
  105.4 25.0 %reduce-scatter.9.cloned.1.call-done = f32[64,512]{1,0:T(8,128)} async-done(((f32[64,1024]{1,0:T(8,128)}), f32[64,512]{1,0:T(8,128)}) %reduce-scatter.9.cloned.1.call-update) | async-done | bytes 131088 | tf_op jit(solution)/shard_map/reduce_scatter | solution.py:177
  130.4 17.4 %all-gather = f32[128,512]{1,0:T(8,128)} all-gather(f32[64,512]{1,0:T(8,128)} %reduce-scatter.9.cloned.1.call-done), channel_id=2, replica_groups=mesh['grp'=2,'gx'=64,'gz'=2] {'grp'}, dimensions={0}, use_global_device_ids=true | all-gather | bytes 393216 | tf_op jit(solution)/shard_map/all_gather | solution.py:178
  151.7 4.9 convolution_bitcast_fusion.6
  156.7 4.9 convolution_bitcast_fusion.7
  165.1 4.0 collective-permute-start.11
  170.6 4.4 collective-permute-start.12
  191.6 15.3 %all-to-all-start.1 = ((f32[64,1,512]{2,1,0:T(1,128)}), f32[64,1,512]{2,1,0:T(1,128)S(1)}, u32[]{:S(2)}, u32[]{:S(2)}) async-start(f32[64,1,512]{2,1,0:T(1,128)} %reshape.595), calls=%async_computation.3 | async-start | bytes 262144 | tf_op jit(solution)/shard_map/all_to_all | solution.py:209
  209.9 9.0 %all-to-all-done.1 = f32[64,1,512]{2,1,0:T(1,128)S(1)} async-done(((f32[64,1,512]{2,1,0:T(1,128)}), f32[64,1,512]{2,1,0:T(1,128)S(1)}, u32[]{:S(2)}, u32[]{:S(2)}) %all-to-all-start.1) | async-done | bytes 131104 | tf_op jit(solution)/shard_map/all_to_all | solution.py:209
  238.1 4.3 copy.256
  242.4 7.4 %reshape.597 = f32[64,1,512]{2,1,0:T(1,128)} reshape(f32[4096,2,4]{2,1,0:T(2,128)} %bitcast.435) | data formatting | bytes 262144
  249.8 4.6 all-to-all-start.2
  266.8 6.2 collective-permute-start.17
  273.9 7.8 %reshape.598 = f32[4096,2,4]{2,1,0:T(2,128)} reshape(f32[64,512]{1,0:T(8,128)S(1)} %reduce.42) | data formatting | bytes 262144
  281.8 5.4 copy.337
  287.3 4.6 fusion.193
  292.0 5.4 convolution_subtract_fusion.2
  302.4 12.9 %reduce-scatter.13.cloned.1.call-done = f32[64,512]{1,0:T(8,128)} async-done(((f32[64,1024]{1,0:T(8,128)}), f32[64,512]{1,0:T(8,128)}) %reduce-scatter.13.cloned.1.call-update) | async-done | bytes 131088 | tf_op jit(solution)/shard_map/reduce_scatter | solution.py:177
  315.3 7.2 all-gather.1
  325.7 5.0 convolution_bitcast_fusion.4
  330.7 4.9 convolution_bitcast_fusion.5
  338.0 4.0 collective-permute-start.20
  355.5 5.4 reduce-scatter.15.cloned.1.call-done
  364.6 12.8 %all-to-all-start.3 = ((f32[64,1,512]{2,1,0:T(1,128)}), f32[64,1,512]{2,1,0:T(1,128)}, u32[]{:S(2)}, u32[]{:S(2)}) async-start(f32[64,1,512]{2,1,0:T(1,128)} %reshape.599), calls=%async_computation.7 | async-start | bytes 262144 | tf_op jit(solution)/shard_map/all_to_all | solution.py:209
  380.8 8.5 %all-to-all-done.3 = f32[64,1,512]{2,1,0:T(1,128)} async-done(((f32[64,1,512]{2,1,0:T(1,128)}), f32[64,1,512]{2,1,0:T(1,128)}, u32[]{:S(2)}, u32[]{:S(2)}) %all-to-all-start.3) | async-done | bytes 131104 | tf_op jit(solution)/shard_map/all_to_all | solution.py:209
  412.9 4.3 copy.272
  417.2 7.4 %reshape.601 = f32[64,1,512]{2,1,0:T(1,128)} reshape(f32[4096,2,4]{2,1,0:T(2,128)} %bitcast.437) | data formatting | bytes 262144
  424.6 4.7 all-to-all-start.4
  441.6 6.2 collective-permute-start.26
  448.7 7.8 %reshape.602 = f32[4096,2,4]{2,1,0:T(2,128)} reshape(f32[64,512]{1,0:T(8,128)S(1)} %reduce.44) | data formatting | bytes 262144
  456.5 5.4 copy.342
  462.1 4.6 fusion.191
  466.7 5.4 convolution_subtract_fusion.1
  477.0 13.1 %reduce-scatter.17.cloned.1.call-done = f32[64,512]{1,0:T(8,128)} async-done(((f32[64,1024]{1,0:T(8,128)}), f32[64,512]{1,0:T(8,128)}) %reduce-scatter.17.cloned.1.call-update) | async-done | bytes 131088 | tf_op jit(solution)/shard_map/reduce_scatter | solution.py:177
  490.1 7.3 all-gather.2
  501.3 5.0 convolution_bitcast_fusion.2
  506.3 4.9 convolution_bitcast_fusion.3
  519.2 4.2 collective-permute-start.30
  529.4 7.1 reduce-scatter.19.cloned.1.call-done
  540.1 12.6 %all-to-all-start.5 = ((f32[64,1,512]{2,1,0:T(1,128)}), f32[64,1,512]{2,1,0:T(1,128)}, u32[]{:S(2)}, u32[]{:S(2)}) async-start(f32[64,1,512]{2,1,0:T(1,128)} %reshape.603), calls=%async_computation.11 | async-start | bytes 262144 | tf_op jit(solution)/shard_map/all_to_all | solution.py:209
  556.0 8.6 %all-to-all-done.5 = f32[64,1,512]{2,1,0:T(1,128)} async-done(((f32[64,1,512]{2,1,0:T(1,128)}), f32[64,1,512]{2,1,0:T(1,128)}, u32[]{:S(2)}, u32[]{:S(2)}) %all-to-all-start.5) | async-done | bytes 131104 | tf_op jit(solution)/shard_map/all_to_all | solution.py:209
  583.2 4.3 copy.288
  587.5 7.6 %reshape.605 = f32[64,1,512]{2,1,0:T(1,128)} reshape(f32[4096,2,4]{2,1,0:T(2,128)} %bitcast.439) | data formatting | bytes 262144
  595.1 5.5 all-to-all-start.6
  603.6 8.3 %all-to-all-done.6 = f32[64,1,512]{2,1,0:T(1,128)} async-done(((f32[64,1,512]{2,1,0:T(1,128)}), f32[64,1,512]{2,1,0:T(1,128)}, u32[]{:S(2)}, u32[]{:S(2)}) %all-to-all-start.6) | async-done | bytes 131104 | tf_op jit(solution)/shard_map/all_to_all | solution.py:173
  613.7 7.8 %reshape.606 = f32[4096,2,4]{2,1,0:T(2,128)} reshape(f32[64,512]{1,0:T(8,128)S(1)} %reduce.46) | data formatting | bytes 262144
  621.6 5.4 copy.347
  627.1 4.6 fusion.189
  631.7 5.4 convolution_subtract_fusion
  646.6 6.0 collective-permute-start.35
  652.6 6.1 all-gather.3
  660.0 5.0 convolution_bitcast_fusion
  664.9 4.9 convolution_bitcast_fusion.1
  672.9 13.8 %reduce-scatter.23.cloned.1.call-done = f32[256,2,64]{0,2,1:T(8,128)} async-done(((f32[512,2,64]{0,2,1:T(8,128)}), f32[256,2,64]{0,2,1:T(8,128)}) %reduce-scatter.23.cloned.1.call-update) | async-done | bytes 131088 | tf_op jit(solution)/shard_map/reduce_scatter | solution.py:206
  688.8 12.6 %all-to-all-start.7 = ((f32[64,1,512]{2,1,0:T(1,128)}), f32[64,1,512]{2,1,0:T(1,128)S(1)}, u32[]{:S(2)}, u32[]{:S(2)}) async-start(f32[64,1,512]{2,1,0:T(1,128)} %reshape.607), calls=%async_computation.15 | async-start | bytes 262144 | tf_op jit(solution)/shard_map/all_to_all | solution.py:209
  707.9 5.5 all-to-all-done.7
  (416 shorter events, 249.8 us)
Async XLA Ops:
  26.7 30.2 %copy-start = (f32[1,4,64,512]{3,2,1,0:T(8,128)S(1)}, f32[1,4,64,512]{3,2,1,0:T(8,128)}, u32[]{:S(2)}) copy-start(f32[1,4,64,512]{3,2,1,0:T(8,128)} %param.19) | copy-start | bytes 1572868
  26.7 50.4 %all-to-all-start = ((f32[64,1,512]{2,1,0:T(1,128)}), f32[64,1,512]{2,1,0:T(1,128)S(1)}, u32[]{:S(2)}, u32[]{:S(2)}) async-start(f32[64,1,512]{2,1,0:T(1,128)} %reshape.593), calls=%async_computation | async-start | bytes 262144 | tf_op jit(solution)/shard_map/all_to_all | solution.py:173
  41.9 88.5 %reduce-scatter.9.cloned.1.call-start = ((), (), s32[]{:S(2)}) async-start(), calls=%async_computation.16 | async-start | bytes 393216 | tf_op jit(solution)/shard_map/reduce_scatter | solution.py:177
  43.1 6.7 collective-permute-start.1
  44.4 5.4 collective-permute-start.2
  49.1 100.4 %collective-permute-start = (f32[64,512]{1,0:T(8,128)}, f32[64,512]{1,0:T(8,128)}, u32[]{:S(2)}, u32[]{:S(2)}) collective-permute-start(f32[64,512]{1,0:T(8,128)} %slice_bitcast_fusion.24), channel_id=1, source_target_pairs={{0,128},{128,0},{1,129},{129,1},{2,130},{130,2},{3,131},{131,3},{4... | collective-permute-start | bytes 393224 | tf_op jit(solution)/shard_map/ppermute | solution.py:33
  49.9 5.0 collective-permute-start.3
  53.7 103.0 %copy-start.47 = (s32[512]{0:T(512)}, s32[512]{0:T(512)S(1)}, u32[]{:S(2)}) copy-start(s32[512]{0:T(512)S(1)} %fusion.468) | copy-start | bytes 6148
  53.7 3.3 collective-permute-start.4
  59.3 147.6 %copy-start.2 = (f32[1,1,4,64,512]{4,3,2,1,0:T(8,128)}, f32[1,1,4,64,512]{4,3,2,1,0:T(8,128)S(1)}, u32[]{:S(2)}) copy-start(f32[1,1,4,64,512]{4,3,2,1,0:T(8,128)S(1)} %get-tuple-element.113) | copy-start | bytes 1572868
  60.6 5.0 collective-permute-start.5
  64.3 4.7 collective-permute-start.6
  65.6 31.0 %copy-start.51 = (s32[256]{0:T(256)}, s32[256]{0:T(256)S(1)}, u32[]{:S(2)}) copy-start(s32[256]{0:T(256)S(1)} %fusion.479) | copy-start | bytes 3076
  70.9 31.2 %collective-permute-start.7 = (f32[2,1,4,68,2]{4,3,2,1,0:T(8,128)}, f32[2,1,4,68,2]{4,3,2,1,0:T(8,128)}, u32[]{:S(2)}, u32[]{:S(2)}) collective-permute-start(f32[2,1,4,68,2]{4,3,2,1,0:T(8,128)} %get-tuple-element.90), channel_id=1, source_target_pairs={{0,1},{2,3},{4,5},{6,7},{8,9},{10,11},{12,13},{14,15},{16,17},{18,... | collective-permute-start | bytes 13064 | tf_op jit(solution)/shard_map/ppermute | solution.py:23
  72.2 29.9 %collective-permute-start.8 = (f32[2,1,4,68,2]{4,3,2,1,0:T(8,128)}, f32[2,1,4,68,2]{4,3,2,1,0:T(8,128)}, u32[]{:S(2)}, u32[]{:S(2)}) collective-permute-start(f32[2,1,4,68,2]{4,3,2,1,0:T(8,128)} %get-tuple-element.91), channel_id=1, source_target_pairs={{1,0},{3,2},{5,4},{7,6},{9,8},{11,10},{13,12},{15,14},{17,16},{19,... | collective-permute-start | bytes 13064 | tf_op jit(solution)/shard_map/ppermute | solution.py:25
  102.0 86.0 %reduce-scatter.11.cloned.1.call-start = ((), (), s32[]{:S(2)}) async-start(), calls=%async_computation.17 | async-start | bytes 393216 | tf_op jit(solution)/shard_map/reduce_scatter | solution.py:206
  102.1 54.6 %copy-start.49 = (s32[512]{0:T(512)}, s32[512]{0:T(512)S(1)}, u32[]{:S(2)}) copy-start(s32[512]{0:T(512)S(1)} %iota_add_fusion) | copy-start | bytes 6148
  104.1 45.3 %copy-start.22 = (f32[64,512]{1,0:T(8,128)S(1)}, f32[64,512]{1,0:T(8,128)}, u32[]{:S(2)}) copy-start(f32[64,512]{1,0:T(8,128)} %param.20) | copy-start | bytes 393220
  104.1 45.3 %copy-start.25 = (f32[64,512]{1,0:T(8,128)S(1)}, f32[64,512]{1,0:T(8,128)}, u32[]{:S(2)}) copy-start(f32[64,512]{1,0:T(8,128)} %param.21) | copy-start | bytes 393220
  163.8 6.0 collective-permute-start.10
  165.1 4.8 collective-permute-start.11
  170.6 10.4 %collective-permute-start.12 = (f32[1,4,68,2]{3,2,1,0:T(8,128)}, f32[1,4,68,2]{3,2,1,0:T(8,128)}, u32[]{:S(2)}, u32[]{:S(2)}) collective-permute-start(f32[1,4,68,2]{3,2,1,0:T(8,128)} %get-tuple-element.110), channel_id=1, source_target_pairs={{1,0},{3,2},{5,4},{7,6},{9,8},{11,10},{13,12},{15,14},{17,16},{19,... | collective-permute-start | bytes 6536 | tf_op jit(solution)/shard_map/ppermute | solution.py:25
  179.7 3.3 collective-permute-start.13
  191.6 27.3 %all-to-all-start.1 = ((f32[64,1,512]{2,1,0:T(1,128)}), f32[64,1,512]{2,1,0:T(1,128)S(1)}, u32[]{:S(2)}, u32[]{:S(2)}) async-start(f32[64,1,512]{2,1,0:T(1,128)} %reshape.595), calls=%async_computation.3 | async-start | bytes 262144 | tf_op jit(solution)/shard_map/all_to_all | solution.py:209
  249.8 23.2 %all-to-all-start.2 = ((f32[64,1,512]{2,1,0:T(1,128)}), f32[64,1,512]{2,1,0:T(1,128)S(1)}, u32[]{:S(2)}, u32[]{:S(2)}) async-start(f32[64,1,512]{2,1,0:T(1,128)} %reshape.597), calls=%async_computation.4 | async-start | bytes 262144 | tf_op jit(solution)/shard_map/all_to_all | solution.py:173
  254.5 60.8 %reduce-scatter.13.cloned.1.call-start = ((), (), s32[]{:S(2)}) async-start(), calls=%async_computation.18 | async-start | bytes 393216 | tf_op jit(solution)/shard_map/reduce_scatter | solution.py:177
  255.5 4.2 collective-permute-start.14
  258.4 5.0 collective-permute-start.15
  265.5 33.6 %collective-permute-start.16 = (f32[2,1,4,68,2]{4,3,2,1,0:T(8,128)}, f32[2,1,4,68,2]{4,3,2,1,0:T(8,128)}, u32[]{:S(2)}, u32[]{:S(2)}) collective-permute-start(f32[2,1,4,68,2]{4,3,2,1,0:T(8,128)} %get-tuple-element.88), channel_id=1, source_target_pairs={{0,1},{2,3},{4,5},{6,7},{8,9},{10,11},{12,13},{14,15},{16,17},{18,... | collective-permute-start | bytes 13064 | tf_op jit(solution)/shard_map/ppermute | solution.py:23
  266.8 32.3 %collective-permute-start.17 = (f32[2,1,4,68,2]{4,3,2,1,0:T(8,128)}, f32[2,1,4,68,2]{4,3,2,1,0:T(8,128)}, u32[]{:S(2)}, u32[]{:S(2)}) collective-permute-start(f32[2,1,4,68,2]{4,3,2,1,0:T(8,128)} %get-tuple-element.89), channel_id=1, source_target_pairs={{1,0},{3,2},{5,4},{7,6},{9,8},{11,10},{13,12},{15,14},{17,16},{19,... | collective-permute-start | bytes 13064 | tf_op jit(solution)/shard_map/ppermute | solution.py:25
  297.4 63.6 %reduce-scatter.15.cloned.1.call-start = ((), (), s32[]{:S(2)}) async-start(), calls=%async_computation.19 | async-start | bytes 393216 | tf_op jit(solution)/shard_map/reduce_scatter | solution.py:206
  298.1 25.4 %collective-permute-start.9 = (f32[64,512]{1,0:T(8,128)}, f32[64,512]{1,0:T(8,128)}, u32[]{:S(2)}, u32[]{:S(2)}) collective-permute-start(f32[64,512]{1,0:T(8,128)} %slice_bitcast_fusion.19), channel_id=1, source_target_pairs={{0,128},{128,0},{1,129},{129,1},{2,130},{130,2},{3,131},{131,3},{4... | collective-permute-start | bytes 393224 | tf_op jit(solution)/shard_map/ppermute | solution.py:33
  301.2 24.5 %copy-start.48 = (s32[512]{0:T(512)S(1)}, s32[512]{0:T(512)}, u32[]{:S(2)}) copy-start(s32[512]{0:T(512)} %copy-done.47) | copy-start | bytes 6148
  301.2 24.5 %copy-start.50 = (s32[512]{0:T(512)S(1)}, s32[512]{0:T(512)}, u32[]{:S(2)}) copy-start(s32[512]{0:T(512)} %copy-done.49) | copy-start | bytes 6148
  336.7 6.0 collective-permute-start.19
  338.0 4.8 collective-permute-start.20
  343.0 8.8 %collective-permute-start.21 = (f32[1,4,68,2]{3,2,1,0:T(8,128)S(1)}, f32[1,4,68,2]{3,2,1,0:T(8,128)S(1)}, u32[]{:S(2)}, u32[]{:S(2)}) collective-permute-start(f32[1,4,68,2]{3,2,1,0:T(8,128)S(1)} %get-tuple-element.106), channel_id=1, source_target_pairs={{1,0},{3,2},{5,4},{7,6},{9,8},{11,10},{13,12},{15,14},{17,16},{19,... | collective-permute-start | bytes 6536 | tf_op jit(solution)/shard_map/ppermute | solution.py:25
  350.5 3.3 collective-permute-start.22
  351.9 25.5 %copy-start.3 = (f32[1,1,4,64,512]{4,3,2,1,0:T(8,128)S(1)}, f32[1,1,4,64,512]{4,3,2,1,0:T(8,128)}, u32[]{:S(2)}) copy-start(f32[1,1,4,64,512]{4,3,2,1,0:T(8,128)} %copy-done.2) | copy-start | bytes 1572868
  364.6 24.7 %all-to-all-start.3 = ((f32[64,1,512]{2,1,0:T(1,128)}), f32[64,1,512]{2,1,0:T(1,128)}, u32[]{:S(2)}, u32[]{:S(2)}) async-start(f32[64,1,512]{2,1,0:T(1,128)} %reshape.599), calls=%async_computation.7 | async-start | bytes 262144 | tf_op jit(solution)/shard_map/all_to_all | solution.py:209
  424.6 23.1 %all-to-all-start.4 = ((f32[64,1,512]{2,1,0:T(1,128)}), f32[64,1,512]{2,1,0:T(1,128)S(1)}, u32[]{:S(2)}, u32[]{:S(2)}) async-start(f32[64,1,512]{2,1,0:T(1,128)} %reshape.601), calls=%async_computation.8 | async-start | bytes 262144 | tf_op jit(solution)/shard_map/all_to_all | solution.py:173
  429.3 60.8 %reduce-scatter.17.cloned.1.call-start = ((), (), s32[]{:S(2)}) async-start(), calls=%async_computation.20 | async-start | bytes 393216 | tf_op jit(solution)/shard_map/reduce_scatter | solution.py:177
  430.4 4.2 collective-permute-start.23
  433.3 5.0 collective-permute-start.24
  440.3 33.5 %collective-permute-start.25 = (f32[2,1,4,68,2]{4,3,2,1,0:T(8,128)}, f32[2,1,4,68,2]{4,3,2,1,0:T(8,128)}, u32[]{:S(2)}, u32[]{:S(2)}) collective-permute-start(f32[2,1,4,68,2]{4,3,2,1,0:T(8,128)} %get-tuple-element.86), channel_id=1, source_target_pairs={{0,1},{2,3},{4,5},{6,7},{8,9},{10,11},{12,13},{14,15},{16,17},{18,... | collective-permute-start | bytes 13064 | tf_op jit(solution)/shard_map/ppermute | solution.py:23
  441.6 32.2 %collective-permute-start.26 = (f32[2,1,4,68,2]{4,3,2,1,0:T(8,128)}, f32[2,1,4,68,2]{4,3,2,1,0:T(8,128)}, u32[]{:S(2)}, u32[]{:S(2)}) collective-permute-start(f32[2,1,4,68,2]{4,3,2,1,0:T(8,128)} %get-tuple-element.87), channel_id=1, source_target_pairs={{1,0},{3,2},{5,4},{7,6},{9,8},{11,10},{13,12},{15,14},{17,16},{19,... | collective-permute-start | bytes 13064 | tf_op jit(solution)/shard_map/ppermute | solution.py:25
  472.1 64.4 %reduce-scatter.19.cloned.1.call-start = ((), (), s32[]{:S(2)}) async-start(), calls=%async_computation.21 | async-start | bytes 393216 | tf_op jit(solution)/shard_map/reduce_scatter | solution.py:206
  472.8 26.2 %collective-permute-start.18 = (f32[64,512]{1,0:T(8,128)}, f32[64,512]{1,0:T(8,128)}, u32[]{:S(2)}, u32[]{:S(2)}) collective-permute-start(f32[64,512]{1,0:T(8,128)} %slice_bitcast_fusion.14), channel_id=1, source_target_pairs={{0,128},{128,0},{1,129},{129,1},{2,130},{130,2},{3,131},{131,3},{4... | collective-permute-start | bytes 393224 | tf_op jit(solution)/shard_map/ppermute | solution.py:33
  512.3 6.1 collective-permute-start.28
  513.6 4.8 collective-permute-start.29
  519.2 9.2 %collective-permute-start.30 = (f32[1,4,68,2]{3,2,1,0:T(8,128)S(1)}, f32[1,4,68,2]{3,2,1,0:T(8,128)S(1)}, u32[]{:S(2)}, u32[]{:S(2)}) collective-permute-start(f32[1,4,68,2]{3,2,1,0:T(8,128)S(1)} %get-tuple-element.102), channel_id=1, source_target_pairs={{1,0},{3,2},{5,4},{7,6},{9,8},{11,10},{13,12},{15,14},{17,16},{19,... | collective-permute-start | bytes 6536 | tf_op jit(solution)/shard_map/ppermute | solution.py:25
  527.0 25.7 %copy-start.18 = (f32[1,4,64,512]{3,2,1,0:T(8,128)S(1)}, f32[1,4,64,512]{3,2,1,0:T(8,128)}, u32[]{:S(2)}) copy-start(f32[1,4,64,512]{3,2,1,0:T(8,128)} %get-tuple-element.69) | copy-start | bytes 1572868
  527.0 25.7 %collective-permute-start.31 = (f32[1,4,68,2]{3,2,1,0:T(8,128)}, f32[1,4,68,2]{3,2,1,0:T(8,128)}, u32[]{:S(2)}, u32[]{:S(2)}) collective-permute-start(f32[1,4,68,2]{3,2,1,0:T(8,128)} %get-tuple-element.103), channel_id=1, source_target_pairs={{0,1},{2,3},{4,5},{6,7},{8,9},{10,11},{12,13},{14,15},{16,17},{18,... | collective-permute-start | bytes 6536 | tf_op jit(solution)/shard_map/ppermute | solution.py:23
  540.1 24.5 %all-to-all-start.5 = ((f32[64,1,512]{2,1,0:T(1,128)}), f32[64,1,512]{2,1,0:T(1,128)}, u32[]{:S(2)}, u32[]{:S(2)}) async-start(f32[64,1,512]{2,1,0:T(1,128)} %reshape.603), calls=%async_computation.11 | async-start | bytes 262144 | tf_op jit(solution)/shard_map/all_to_all | solution.py:209
  595.1 16.8 %all-to-all-start.6 = ((f32[64,1,512]{2,1,0:T(1,128)}), f32[64,1,512]{2,1,0:T(1,128)}, u32[]{:S(2)}, u32[]{:S(2)}) async-start(f32[64,1,512]{2,1,0:T(1,128)} %reshape.605), calls=%async_computation.12 | async-start | bytes 262144 | tf_op jit(solution)/shard_map/all_to_all | solution.py:173
  600.6 51.9 %reduce-scatter.21.cloned.1.call-start = ((), (), s32[]{:S(2)}) async-start(), calls=%async_computation.22 | async-start | bytes 393216 | tf_op jit(solution)/shard_map/reduce_scatter | solution.py:177
  637.2 49.6 %reduce-scatter.23.cloned.1.call-start = ((), (), s32[]{:S(2)}) async-start(), calls=%async_computation.23 | async-start | bytes 393216 | tf_op jit(solution)/shard_map/reduce_scatter | solution.py:206
  637.2 5.2 collective-permute-start.32
  639.7 4.7 collective-permute-start.33
  641.6 17.0 %collective-permute-start.27 = (f32[64,512]{1,0:T(8,128)}, f32[64,512]{1,0:T(8,128)S(1)}, u32[]{:S(2)}, u32[]{:S(2)}) collective-permute-start(f32[64,512]{1,0:T(8,128)} %slice_bitcast_fusion.9), channel_id=1, source_target_pairs={{0,128},{128,0},{1,129},{129,1},{2,130},{130,2},{3,131},{131,3},{4... | collective-permute-start | bytes 393224 | tf_op jit(solution)/shard_map/ppermute | solution.py:33
  645.3 25.3 %collective-permute-start.34 = (f32[2,1,4,68,2]{4,3,2,1,0:T(8,128)}, f32[2,1,4,68,2]{4,3,2,1,0:T(8,128)S(1)}, u32[]{:S(2)}, u32[]{:S(2)}) collective-permute-start(f32[2,1,4,68,2]{4,3,2,1,0:T(8,128)} %get-tuple-element.84), channel_id=1, source_target_pairs={{0,1},{2,3},{4,5},{6,7},{8,9},{10,11},{12,13},{14,15},{16,17},{18,... | collective-permute-start | bytes 13064 | tf_op jit(solution)/shard_map/ppermute | solution.py:23
  646.6 24.0 %collective-permute-start.35 = (f32[2,1,4,68,2]{4,3,2,1,0:T(8,128)}, f32[2,1,4,68,2]{4,3,2,1,0:T(8,128)S(1)}, u32[]{:S(2)}, u32[]{:S(2)}) collective-permute-start(f32[2,1,4,68,2]{4,3,2,1,0:T(8,128)} %get-tuple-element.85), channel_id=1, source_target_pairs={{1,0},{3,2},{5,4},{7,6},{9,8},{11,10},{13,12},{15,14},{17,16},{19,... | collective-permute-start | bytes 13064 | tf_op jit(solution)/shard_map/ppermute | solution.py:25
  671.3 30.1 %copy-start.15 = (f32[1,4,64,512]{3,2,1,0:T(8,128)S(1)}, f32[1,4,64,512]{3,2,1,0:T(8,128)}, u32[]{:S(2)}) copy-start(f32[1,4,64,512]{3,2,1,0:T(8,128)} %param.18) | copy-start | bytes 1572868
  688.8 24.6 %all-to-all-start.7 = ((f32[64,1,512]{2,1,0:T(1,128)}), f32[64,1,512]{2,1,0:T(1,128)S(1)}, u32[]{:S(2)}, u32[]{:S(2)}) async-start(f32[64,1,512]{2,1,0:T(1,128)} %reshape.607), calls=%async_computation.15 | async-start | bytes 262144 | tf_op jit(solution)/shard_map/all_to_all | solution.py:209
  (41 other events, 395.4 us)
Sparse Core Ops, SparseCore 0:
  102.1 28.2 reduce-scatter.8
  169.9 18.0 reduce-scatter.10
  297.5 17.7 reduce-scatter.12
  342.8 18.0 reduce-scatter.14
  472.2 17.8 reduce-scatter.16
  518.4 18.0 reduce-scatter.18
  637.3 8.9 reduce-scatter.20
  670.7 16.0 reduce-scatter.22
